TPU v7x, 128 devices: a whole 4x4x4 slice. The times are simulated.
128 devices in a mesh: section: 8 (over y, core), dom: 16 (over z, x).
Axes of the slice: x: 4, y: 4, z: 4, core: 2. Of those that a mesh axis runs over, the one named last changes fastest.
Arguments:
- carry_h: bfloat16 [8, 16384, 512], P('section', 'dom'), may hold values from -6 to 6
- carry_h0: bfloat16 [8, 16384, 512], P('section', 'dom'), may hold values from -6 to 6
- new_h0: bfloat16 [3, 16384, 512], P(None, 'dom'), may hold values from -6 to 6
- weights: bfloat16 [8, 512, 512], P('section'), may hold values from -0.25 to 0.25
- adj_blocks: bfloat16 [128, 24, 128, 128], P('dom'), may hold values from -0.109375 to 0.109375
- col_index: int32 [128, 24], P('dom'), may hold values from 0 to 23
- counts: int32 [128], P('dom'), may hold values from 1 to 24, as said below
- send_list: int32 [16, 16], replicated, may hold values from 0 to 7
Outputs:
- layer_out: bfloat16 [8, 4, 16384, 512], P('section', None, 'dom')
Inputs may be any that keep to these rules, and one draw needn't show every extreme that they name: `counts`: every graph part has a row block with exactly 24 live blocks; parts differ in their mean load.
All inputs are finite; a program needn't handle non-finite values.
Results may differ from a plain program's by a relative error of at most 0.0052.
Values may be sent and summed in bfloat16 or wider, within the bound.
A program may use at most 128 MiB of HBM per device.

v0:
```python
import jax
import jax.numpy as jnp
from jax import lax
from jax.sharding import PartitionSpec as P

BLOCK = 128
STEPS = 4


teleport = 0.2
strength = 1.5


def shifted_2(value, axis, by):
    length = lax.axis_size(axis)
    pairs = [(i, i + by) for i in range(length) if 0 <= i + by < length]
    return lax.ppermute(value, axis, pairs)


def body(carry_h, carry_h0, new_h0, weights, adj_blocks, col_index, counts, send_list):
    section_pos = lax.axis_index("section")
    part_index = lax.axis_index("dom")
    row_count = carry_h.shape[1]
    feature_width = carry_h.shape[2]
    block_count = row_count // BLOCK
    weight = weights[0]
    layer_beta = jnp.log(1.0 + strength / (section_pos.astype(jnp.float32) + 1.0))
    slot_ids = jnp.arange(adj_blocks.shape[1])
    live_slots = slot_ids[None, :] < counts[:, None]
    masked_adj = jnp.where(
        live_slots[:, :, None, None], adj_blocks, jnp.zeros((), adj_blocks.dtype)
    )
    outgoing_ids = lax.dynamic_index_in_dim(send_list, part_index, 0, keepdims=False)
    first_section = section_pos == 0
    current = carry_h[0]
    anchor = carry_h0[0]
    results = []
    delayed = [carry_h0[0]]
    for step_lag in range(1, STEPS):
        delayed.append(shifted_2(carry_h0[0], "section", step_lag))
    for step in range(STEPS):
        if step > 0:
            shifted = shifted_2(results[-1], "section", 1)
            current = jnp.where(first_section, new_h0[step - 1], shifted)
            fresh_index = jnp.clip(step - section_pos - 1, 0, new_h0.shape[0] - 1)
            fresh_anchor = lax.dynamic_index_in_dim(new_h0, fresh_index, 0, keepdims=False)
            anchor = jnp.where(section_pos >= step, delayed[step], fresh_anchor)
        own_blocks = current.reshape(block_count, BLOCK, feature_width)
        outgoing = jnp.take(own_blocks, outgoing_ids, axis=0)
        incoming = lax.all_to_all(outgoing, "dom", split_axis=0, concat_axis=0, tiled=True)
        lookup = jnp.concatenate([own_blocks, incoming], axis=0)
        picked = jnp.take(lookup, col_index, axis=0)
        gathered = jnp.einsum(
            "rkij,rkjd->rid", masked_adj, picked, preferred_element_type=jnp.float32
        )
        gathered = gathered.reshape(row_count, feature_width)
        mixture = ((1.0 - teleport) * gathered + teleport * anchor.astype(jnp.float32)).astype(
            jnp.bfloat16
        )
        product = jnp.dot(mixture, weight, preferred_element_type=jnp.float32)
        results.append(
            jax.nn.relu(
                (1.0 - layer_beta) * mixture.astype(jnp.float32) + layer_beta * product
            ).astype(jnp.bfloat16)
        )
    return jnp.stack(results)[None]


def solution(mesh):
    in_specs = (
        P("section", "dom", None),
        P("section", "dom", None),
        P(None, "dom", None),
        P("section", None, None),
        P("dom", None, None, None),
        P("dom", None),
        P("dom"),
        P(),
    )
    out_specs = P("section", None, "dom", None)
    return jax.shard_map(body, mesh=mesh, in_specs=in_specs, out_specs=out_specs, check_vma=False)
```

profile of v0, /device:TPU:16, one launch (start us, length us, event | category | flops | bytes accessed | tf_op | source)
XLA Modules:
  0.0 340.7 jit_solution(7854461876847068394)
XLA Ops:
  0.8 1.9 gather_fusion
  2.7 1.6 broadcast_select_fusion.8
  4.3 8.1 %all-to-all-start = ((bf16[16,128,512]{2,1,0:T(8,128)(2,1)}), bf16[16,128,512]{2,1,0:T(8,128)(2,1)}, u32[]{:S(2)}, u32[]{:S(2)}) async-start(bf16[16,128,512]{2,1,0:T(8,128)(2,1)} %broadcast_select_fusion.8), calls=%async_computation | async-start | bytes 4194304 | tf_op jit(solution)/shard_map/all_to_all | solution.py:50
  12.6 1.7 convert_multiply_fusion
  14.3 29.8 %all-to-all-done = bf16[16,128,512]{2,1,0:T(8,128)(2,1)} async-done(((bf16[16,128,512]{2,1,0:T(8,128)(2,1)}), bf16[16,128,512]{2,1,0:T(8,128)(2,1)}, u32[]{:S(2)}, u32[]{:S(2)}) %all-to-all-start) | async-done | bytes 2097184 | tf_op jit(solution)/shard_map/all_to_all | solution.py:50
  44.2 3.5 %pad_maximum_fusion = bf16[24,128,512]{2,1,0:T(8,128)(2,1)} fusion(bf16[16,128,512]{2,1,0:T(8,128)(2,1)} %all-to-all-done, bf16[8,128,512]{2,1,0:T(8,128)(2,1)S(1)} %bitcast.94), kind=kLoop, calls=%fused_computation.26 | loop fusion | flops 1572864 | bytes 6291456 | tf_op jit(solution)/shard_map/concatenate | solution.py:51
  47.7 13.1 %gather_fusion.1 = bf16[192,128,512]{2,1,0:T(8,128)(2,1)} fusion(bf16[24,128,512]{2,1,0:T(8,128)(2,1)} %pad_maximum_fusion, s32[1024]{0:T(1024)S(1)} %pad_clamp_fusion), kind=kCustom, calls=%fused_computation.1.clone | custom fusion | bytes 50332416 | tf_op jit(solution)/shard_map/jit(_take)/gather | solution.py:52
  60.8 14.3 %add_convert_fusion = (bf16[8,128,512]{2,1,0:T(8,128)(2,1)}, f32[8,128,512]{2,1,0:T(8,128)}) fusion(f32[8,128,512]{2,1,0:T(8,128)} %bitcast.98, bf16[8,24,128,512]{3,2,1,0:T(8,128)(2,1)} %bitcast.83, pred[8,24]{1,0:T(8,128)(4,1)S(1)} %get-tuple-element.12, bf16[8,24,128,128]{3,2,1,0:T(8,128)(2,1)} %param.16, pred[8,24]{1,0:T(8,128)(4,1)S(1)} %get-tuple-element.11), kind=kOutput, calls=%fused_computation.50 | convolution fusion | flops 3238526976 | bytes 36700544 | tf_op jit(solution)/shard_map/rkij,rkjd->rid/dot_general | solution.py:53
  75.0 2.0 fusion.23
  77.1 0.8 maximum_convert_fusion.3
  77.9 1.9 collective-permute-start
  79.8 14.3 %collective-permute-done = bf16[1024,512]{1,0:T(8,128)(2,1)} collective-permute-done((bf16[1024,512]{1,0:T(8,128)(2,1)S(1)}, bf16[1024,512]{1,0:T(8,128)(2,1)}, u32[]{:S(2)}, u32[]{:S(2)}) %collective-permute-start) | collective-permute-done | bytes 1048608 | tf_op jit(solution)/shard_map/ppermute | solution.py:17
  94.1 1.7 bitcast_select_fusion.5
  95.8 2.0 gather_fusion.2
  97.8 3.2 broadcast_select_fusion.7
  101.0 4.4 %all-to-all-start.1 = ((bf16[16,128,512]{2,1,0:T(8,128)(2,1)}), bf16[16,128,512]{2,1,0:T(8,128)(2,1)}, u32[]{:S(2)}, u32[]{:S(2)}) async-start(bf16[16,128,512]{2,1,0:T(8,128)(2,1)} %broadcast_select_fusion.7), calls=%async_computation.1 | async-start | bytes 4194304 | tf_op jit(solution)/shard_map/all_to_all | solution.py:50
  105.4 1.9 collective-permute-start.1
  107.3 28.1 %all-to-all-done.1 = bf16[16,128,512]{2,1,0:T(8,128)(2,1)} async-done(((bf16[16,128,512]{2,1,0:T(8,128)(2,1)}), bf16[16,128,512]{2,1,0:T(8,128)(2,1)}, u32[]{:S(2)}, u32[]{:S(2)}) %all-to-all-start.1) | async-done | bytes 2097184 | tf_op jit(solution)/shard_map/all_to_all | solution.py:50
  135.5 3.5 %pad_maximum_fusion.1 = bf16[24,128,512]{2,1,0:T(8,128)(2,1)} fusion(bf16[16,128,512]{2,1,0:T(8,128)(2,1)} %all-to-all-done.1, bf16[8,128,512]{2,1,0:T(8,128)(2,1)S(1)} %bitcast.92), kind=kLoop, calls=%fused_computation.27 | loop fusion | flops 1572864 | bytes 6291456 | tf_op jit(solution)/shard_map/concatenate | solution.py:51
  139.0 13.1 %gather_fusion.3 = bf16[192,128,512]{2,1,0:T(8,128)(2,1)} fusion(bf16[24,128,512]{2,1,0:T(8,128)(2,1)} %pad_maximum_fusion.1, s32[1024]{0:T(1024)S(1)} %pad_clamp_fusion), kind=kCustom, calls=%fused_computation.5.clone | custom fusion | bytes 50332416 | tf_op jit(solution)/shard_map/jit(_take)/gather | solution.py:52
  152.1 13.6 %bitcast_multiply_fusion.2 = f32[8,128,512]{2,1,0:T(8,128)} fusion(bf16[8,24,128,512]{3,2,1,0:T(8,128)(2,1)} %bitcast.85, pred[8,24]{1,0:T(8,128)(4,1)S(1)} %get-tuple-element.12, bf16[8,24,128,128]{3,2,1,0:T(8,128)(2,1)} %param.16, pred[8,24]{1,0:T(8,128)(4,1)S(1)} %get-tuple-element.11), kind=kOutput, calls=%fused_computation.42 | convolution fusion | flops 3237478400 | bytes 33554816 | tf_op jit(solution)/shard_map/rkij,rkjd->rid/dot_general | solution.py:53
  165.7 2.3 fusion.22
  168.0 0.8 maximum_convert_fusion.2
  168.8 1.9 collective-permute-start.2
  170.7 14.2 %collective-permute-done.2 = bf16[1024,512]{1,0:T(8,128)(2,1)S(1)} collective-permute-done((bf16[1024,512]{1,0:T(8,128)(2,1)S(1)}, bf16[1024,512]{1,0:T(8,128)(2,1)S(1)}, u32[]{:S(2)}, u32[]{:S(2)}) %collective-permute-start.2) | collective-permute-done | bytes 1048608 | tf_op jit(solution)/shard_map/ppermute | solution.py:17
  185.0 2.0 gather_fusion.4
  187.0 3.2 broadcast_select_fusion.6
  190.2 4.4 %all-to-all-start.2 = ((bf16[16,128,512]{2,1,0:T(8,128)(2,1)}), bf16[16,128,512]{2,1,0:T(8,128)(2,1)}, u32[]{:S(2)}, u32[]{:S(2)}) async-start(bf16[16,128,512]{2,1,0:T(8,128)(2,1)} %broadcast_select_fusion.6), calls=%async_computation.2 | async-start | bytes 4194304 | tf_op jit(solution)/shard_map/all_to_all | solution.py:50
  194.7 2.1 collective-permute-start.3
  196.8 25.1 %all-to-all-done.2 = bf16[16,128,512]{2,1,0:T(8,128)(2,1)} async-done(((bf16[16,128,512]{2,1,0:T(8,128)(2,1)}), bf16[16,128,512]{2,1,0:T(8,128)(2,1)}, u32[]{:S(2)}, u32[]{:S(2)}) %all-to-all-start.2) | async-done | bytes 2097184 | tf_op jit(solution)/shard_map/all_to_all | solution.py:50
  221.9 3.5 %pad_maximum_fusion.2 = bf16[24,128,512]{2,1,0:T(8,128)(2,1)} fusion(bf16[16,128,512]{2,1,0:T(8,128)(2,1)} %all-to-all-done.2, bf16[8,128,512]{2,1,0:T(8,128)(2,1)S(1)} %bitcast.90), kind=kLoop, calls=%fused_computation.28 | loop fusion | flops 1572864 | bytes 6291456 | tf_op jit(solution)/shard_map/concatenate | solution.py:51
  225.4 13.1 %gather_fusion.5 = bf16[192,128,512]{2,1,0:T(8,128)(2,1)} fusion(bf16[24,128,512]{2,1,0:T(8,128)(2,1)} %pad_maximum_fusion.2, s32[1024]{0:T(1024)S(1)} %pad_clamp_fusion), kind=kCustom, calls=%fused_computation.6.clone | custom fusion | bytes 50332416 | tf_op jit(solution)/shard_map/jit(_take)/gather | solution.py:52
  238.4 13.6 %bitcast_multiply_fusion.1 = f32[8,128,512]{2,1,0:T(8,128)} fusion(bf16[8,24,128,512]{3,2,1,0:T(8,128)(2,1)} %bitcast.86, pred[8,24]{1,0:T(8,128)(4,1)S(1)} %get-tuple-element.12, bf16[8,24,128,128]{3,2,1,0:T(8,128)(2,1)} %param.16, pred[8,24]{1,0:T(8,128)(4,1)S(1)} %get-tuple-element.11), kind=kOutput, calls=%fused_computation.39 | convolution fusion | flops 3237478400 | bytes 33554816 | tf_op jit(solution)/shard_map/rkij,rkjd->rid/dot_general | solution.py:53
  252.0 2.3 fusion.21
  254.4 0.8 maximum_convert_fusion.1
  255.2 1.9 collective-permute-start.4
  257.1 14.2 %collective-permute-done.4 = bf16[1024,512]{1,0:T(8,128)(2,1)S(1)} collective-permute-done((bf16[1024,512]{1,0:T(8,128)(2,1)S(1)}, bf16[1024,512]{1,0:T(8,128)(2,1)S(1)}, u32[]{:S(2)}, u32[]{:S(2)}) %collective-permute-start.4) | collective-permute-done | bytes 1048608 | tf_op jit(solution)/shard_map/ppermute | solution.py:17
  271.4 2.0 gather_fusion.6
  273.4 3.2 broadcast_select_fusion.5
  276.6 4.5 %all-to-all-start.3 = ((bf16[16,128,512]{2,1,0:T(8,128)(2,1)}), bf16[16,128,512]{2,1,0:T(8,128)(2,1)}, u32[]{:S(2)}, u32[]{:S(2)}) async-start(bf16[16,128,512]{2,1,0:T(8,128)(2,1)} %broadcast_select_fusion.5), calls=%async_computation.3 | async-start | bytes 4194304 | tf_op jit(solution)/shard_map/all_to_all | solution.py:50
  281.1 1.9 collective-permute-start.5
  283.0 22.7 %all-to-all-done.3 = bf16[16,128,512]{2,1,0:T(8,128)(2,1)} async-done(((bf16[16,128,512]{2,1,0:T(8,128)(2,1)}), bf16[16,128,512]{2,1,0:T(8,128)(2,1)}, u32[]{:S(2)}, u32[]{:S(2)}) %all-to-all-start.3) | async-done | bytes 2097184 | tf_op jit(solution)/shard_map/all_to_all | solution.py:50
  305.7 3.5 %pad_maximum_fusion.3 = bf16[24,128,512]{2,1,0:T(8,128)(2,1)} fusion(bf16[16,128,512]{2,1,0:T(8,128)(2,1)} %all-to-all-done.3, bf16[8,128,512]{2,1,0:T(8,128)(2,1)S(1)} %bitcast.88), kind=kLoop, calls=%fused_computation.29 | loop fusion | flops 1572864 | bytes 6291456 | tf_op jit(solution)/shard_map/concatenate | solution.py:51
  309.2 13.1 %gather_fusion.7 = bf16[192,128,512]{2,1,0:T(8,128)(2,1)} fusion(bf16[24,128,512]{2,1,0:T(8,128)(2,1)} %pad_maximum_fusion.3, s32[1024]{0:T(1024)S(1)} %pad_clamp_fusion), kind=kCustom, calls=%fused_computation.7.clone | custom fusion | bytes 50332416 | tf_op jit(solution)/shard_map/jit(_take)/gather | solution.py:52
  322.2 12.1 %bitcast_multiply_fusion = f32[8,128,512]{2,1,0:T(8,128)S(1)} fusion(bf16[8,24,128,512]{3,2,1,0:T(8,128)(2,1)} %bitcast.84, pred[8,24]{1,0:T(8,128)(4,1)S(1)} %get-tuple-element.12, bf16[8,24,128,128]{3,2,1,0:T(8,128)(2,1)} %param.16, pred[8,24]{1,0:T(8,128)(4,1)S(1)} %get-tuple-element.11), kind=kOutput, calls=%fused_computation.36 | convolution fusion | flops 3237478400 | bytes 33554816 | tf_op jit(solution)/shard_map/rkij,rkjd->rid/dot_general | solution.py:53
  334.4 2.2 fusion.20
  336.6 0.8 fusion.32
  338.4 2.3 maximum_bitcast_fusion
  (39 shorter events, 2.3 us)
Async XLA Ops:
  0.0 77.1 %copy-start = (bf16[1,512,512]{2,1,0:T(8,128)(2,1)S(1)}, bf16[1,512,512]{2,1,0:T(8,128)(2,1)}, u32[]{:S(2)}) copy-start(bf16[1,512,512]{2,1,0:T(8,128)(2,1)} %param.15) | copy-start | bytes 1572868
  4.3 8.1 %copy-start.11 = (s32[8,24]{1,0:T(8,128)S(1)}, s32[8,24]{1,0:T(8,128)}, u32[]{:S(2)}) copy-start(s32[8,24]{1,0:T(8,128)} %param.17) | copy-start | bytes 2308
  4.3 8.3 %copy-start.12 = (s32[8]{0:T(128)S(1)}, s32[8]{0:T(128)}, u32[]{:S(2)}) copy-start(s32[8]{0:T(128)} %param.18) | copy-start | bytes 100
  4.3 8.4 %copy-start.4 = (bf16[1,1024,512]{2,1,0:T(8,128)(2,1)S(1)}, bf16[1,1024,512]{2,1,0:T(8,128)(2,1)}, u32[]{:S(2)}) copy-start(bf16[1,1024,512]{2,1,0:T(8,128)(2,1)} %param.13) | copy-start | bytes 3145732
  4.3 39.9 %all-to-all-start = ((bf16[16,128,512]{2,1,0:T(8,128)(2,1)}), bf16[16,128,512]{2,1,0:T(8,128)(2,1)}, u32[]{:S(2)}, u32[]{:S(2)}) async-start(bf16[16,128,512]{2,1,0:T(8,128)(2,1)} %broadcast_select_fusion.8), calls=%async_computation | async-start | bytes 4194304 | tf_op jit(solution)/shard_map/all_to_all | solution.py:50
  12.4 31.8 %copy-start.3 = (bf16[1,1024,512]{2,1,0:T(8,128)(2,1)S(1)}, bf16[1,1024,512]{2,1,0:T(8,128)(2,1)}, u32[]{:S(2)}) copy-start(bf16[1,1024,512]{2,1,0:T(8,128)(2,1)} %param.12) | copy-start | bytes 3145732
  75.0 2.0 copy-start.13
  77.9 1.9 copy-start.5
  77.9 16.2 %collective-permute-start = (bf16[1024,512]{1,0:T(8,128)(2,1)S(1)}, bf16[1024,512]{1,0:T(8,128)(2,1)}, u32[]{:S(2)}, u32[]{:S(2)}) collective-permute-start(bf16[1024,512]{1,0:T(8,128)(2,1)S(1)} %maximum_convert_fusion.3), channel_id=1, source_target_pairs={{0,16},{16,32},{32,48},{48,64},{64,80},{80,96},{96,112},{1,17},{17... | collective-permute-start | bytes 3145736 | tf_op jit(solution)/shard_map/ppermute | solution.py:17
  101.0 34.5 %all-to-all-start.1 = ((bf16[16,128,512]{2,1,0:T(8,128)(2,1)}), bf16[16,128,512]{2,1,0:T(8,128)(2,1)}, u32[]{:S(2)}, u32[]{:S(2)}) async-start(bf16[16,128,512]{2,1,0:T(8,128)(2,1)} %broadcast_select_fusion.7), calls=%async_computation.1 | async-start | bytes 4194304 | tf_op jit(solution)/shard_map/all_to_all | solution.py:50
  105.4 60.2 %collective-permute-start.1 = (bf16[1024,512]{1,0:T(8,128)(2,1)S(1)}, bf16[1024,512]{1,0:T(8,128)(2,1)}, u32[]{:S(2)}, u32[]{:S(2)}) collective-permute-start(bf16[1024,512]{1,0:T(8,128)(2,1)S(1)} %bitcast.95), channel_id=1, source_target_pairs={{0,16},{16,32},{32,48},{48,64},{64,80},{80,96},{96,112},{1,17},{17... | collective-permute-start | bytes 3145736 | tf_op jit(solution)/shard_map/ppermute | solution.py:17
  152.1 13.6 %copy-start.1 = (bf16[3,1024,512]{2,1,0:T(8,128)(2,1)S(1)}, bf16[3,1024,512]{2,1,0:T(8,128)(2,1)}, u32[]{:S(2)}) copy-start(bf16[3,1024,512]{2,1,0:T(8,128)(2,1)} %param.14) | copy-start | bytes 9437188
  168.8 1.9 copy-start.7
  168.8 16.1 %collective-permute-start.2 = (bf16[1024,512]{1,0:T(8,128)(2,1)S(1)}, bf16[1024,512]{1,0:T(8,128)(2,1)S(1)}, u32[]{:S(2)}, u32[]{:S(2)}) collective-permute-start(bf16[1024,512]{1,0:T(8,128)(2,1)S(1)} %maximum_convert_fusion.2), channel_id=1, source_target_pairs={{0,16},{16,32},{32,48},{48,64},{64,80},{80,96},{96,112},{1,17},{17... | collective-permute-start | bytes 3145736 | tf_op jit(solution)/shard_map/ppermute | solution.py:17
  190.2 31.6 %all-to-all-start.2 = ((bf16[16,128,512]{2,1,0:T(8,128)(2,1)}), bf16[16,128,512]{2,1,0:T(8,128)(2,1)}, u32[]{:S(2)}, u32[]{:S(2)}) async-start(bf16[16,128,512]{2,1,0:T(8,128)(2,1)} %broadcast_select_fusion.6), calls=%async_computation.2 | async-start | bytes 4194304 | tf_op jit(solution)/shard_map/all_to_all | solution.py:50
  194.7 57.4 %collective-permute-start.3 = (bf16[1024,512]{1,0:T(8,128)(2,1)S(1)}, bf16[1024,512]{1,0:T(8,128)(2,1)}, u32[]{:S(2)}, u32[]{:S(2)}) collective-permute-start(bf16[1024,512]{1,0:T(8,128)(2,1)S(1)} %bitcast.96), channel_id=1, source_target_pairs={{0,32},{16,48},{32,64},{48,80},{64,96},{80,112},{1,33},{17,49},{33... | collective-permute-start | bytes 3145736 | tf_op jit(solution)/shard_map/ppermute | solution.py:17
  238.4 13.6 %copy-start.2 = (bf16[3,1024,512]{2,1,0:T(8,128)(2,1)S(1)}, bf16[3,1024,512]{2,1,0:T(8,128)(2,1)}, u32[]{:S(2)}) copy-start(bf16[3,1024,512]{2,1,0:T(8,128)(2,1)} %param.14) | copy-start | bytes 9437188
  255.1 1.9 copy-start.9
  255.2 16.1 %collective-permute-start.4 = (bf16[1024,512]{1,0:T(8,128)(2,1)S(1)}, bf16[1024,512]{1,0:T(8,128)(2,1)S(1)}, u32[]{:S(2)}, u32[]{:S(2)}) collective-permute-start(bf16[1024,512]{1,0:T(8,128)(2,1)S(1)} %maximum_convert_fusion.1), channel_id=1, source_target_pairs={{0,16},{16,32},{32,48},{48,64},{64,80},{80,96},{96,112},{1,17},{17... | collective-permute-start | bytes 3145736 | tf_op jit(solution)/shard_map/ppermute | solution.py:17
  276.6 29.1 %all-to-all-start.3 = ((bf16[16,128,512]{2,1,0:T(8,128)(2,1)}), bf16[16,128,512]{2,1,0:T(8,128)(2,1)}, u32[]{:S(2)}, u32[]{:S(2)}) async-start(bf16[16,128,512]{2,1,0:T(8,128)(2,1)} %broadcast_select_fusion.5), calls=%async_computation.3 | async-start | bytes 4194304 | tf_op jit(solution)/shard_map/all_to_all | solution.py:50
  281.1 53.3 %collective-permute-start.5 = (bf16[1024,512]{1,0:T(8,128)(2,1)S(1)}, bf16[1024,512]{1,0:T(8,128)(2,1)}, u32[]{:S(2)}, u32[]{:S(2)}) collective-permute-start(bf16[1024,512]{1,0:T(8,128)(2,1)S(1)} %bitcast.97), channel_id=1, source_target_pairs={{0,48},{16,64},{32,80},{48,96},{64,112},{1,49},{17,65},{33,81},{49... | collective-permute-start | bytes 3145736 | tf_op jit(solution)/shard_map/ppermute | solution.py:17
  336.6 1.2 copy-start.6
  336.6 1.5 copy-start.8
  336.6 1.8 copy-start.10
where the time goes:
time: 347 us; the launch traced here: 341 us
  waiting for transfers between devices  148 us (43%)
  local copies, waits for them, and re-layouts  61.3 us (18%)
  matrix products  56.6 us (16%)
  other arithmetic  40.9 us (12%)
  starting transfers between devices  33.1 us (10%)
    all_to_all x4, waiting for transfers between devices, body(): lax.all_to_all(outgoing, 'dom', split_axis=0, concat_axis=0, tiled=True)  106 us
    dot_general x4, matrix products, body(): jnp.einsum('rkij,rkjd->rid', masked_adj, picked, preferred_element_type=j...  53.5 us
    gather x4, local copies, waits for them, and re-layouts, body(): picked = jnp.take(lookup, col_index, axis=0)  52.2 us
    ppermute x6, waiting for transfers between devices, shifted_2(): return lax.ppermute(value, axis, pairs)  42.6 us
    all_to_all x4, starting transfers between devices, body(): lax.all_to_all(outgoing, 'dom', split_axis=0, concat_axis=0, tiled=True)  21.4 us
    concatenate x4, other arithmetic, body(): lookup = jnp.concatenate([own_blocks, incoming], axis=0)  14.1 us
    ppermute x6, starting transfers between devices, shifted_2(): return lax.ppermute(value, axis, pairs)  11.7 us
    select_n x4, other arithmetic, body(): outgoing = jnp.take(own_blocks, outgoing_ids, axis=0)  11.1 us
  transfers between devices with their start and end apart: 10, of which 7 were waited for; matrix products, arithmetic and copies ran while one was open for 27% of the time, Pallas kernels for 0%

commit v1 on v0

v1 whole, which is shorter than its diff:
```python
import functools
import math

import jax
import jax.numpy as jnp
from jax import lax
from jax.experimental import pallas as pl
from jax.experimental.pallas import tpu as pltpu
from jax.sharding import PartitionSpec as P

BLOCK = 128
STEPS = 4
TELEPORT = 0.2
STRENGTH = 1.5
MESH = pl.DeviceIdType.MESH

ORDER = (
    (1, 1), (-1, -1),
    (1, -1), (-1, 1),
    (1, 2), (-1, 0),
    (1, 0), (-1, 2),
    (2, 2),
    (2, 0), (0, 2),
    (2, 1), (0, -1),
    (2, -1), (0, 1),
)
PEERS = len(ORDER)


def kernel(
    n_section, n_x, n_z,
    col, counts, send_list, betas, carry_h, carry_h0, new_h0, weights, adj,
    out,
    own0, own1, own2, own3, table0, table1, table2, table3, outgoing, held, result, adjacency, weight,
    token, load_sem, feed_sem, adj_sem, own_sem, send_sem, recv_sem, ship_send, ship_recv, held_send, held_recv, out_sem,
):
    section = lax.axis_index("section")
    part = lax.axis_index("dom")
    z, x = part // n_x, part % n_x
    core = section % 2
    owns = (own0, own1, own2, own3)
    tables = (table0, table1, table2, table3)
    blocks = own0.shape[0]
    pairs = blocks // 2
    slots = adj.shape[1]

    def at(dx, dz):
        return ((z + dz + n_z) % n_z) * n_x + (x + dx + n_x) % n_x

    def along(by):
        return {"section": (section + by + n_section) % n_section}

    barrier = pltpu.get_barrier_semaphore()
    for dx, dz in ORDER:
        pl.semaphore_signal(barrier, inc=1, device_id={"dom": at(dx, dz)}, device_id_type=MESH)
    for by in (1, -1, 2, -2):
        pl.semaphore_signal(barrier, inc=1, device_id=along(by), device_id_type=MESH)

    load_x = pltpu.make_async_copy(carry_h.at[0], own0, load_sem.at[0])
    load_held = pltpu.make_async_copy(carry_h0.at[0], held.at[0], load_sem.at[1])
    load_weight = pltpu.make_async_copy(weights.at[0], weight, load_sem.at[2])
    load_x.start()
    load_held.start()
    load_weight.start()

    def feed(t, what, target):
        return pltpu.make_async_copy(new_h0.at[t - 1], target, feed_sem.at[what, t])

    @pl.when(section == 0)
    def _():
        for t in range(1, STEPS):
            feed(t, 0, owns[t]).start()
            feed(t, 1, held.at[t]).start()

    load_adj = [
        pltpu.make_async_copy(
            adj.at[:, k], adjacency.at[:, k // 2, :, pl.ds((k % 2) * BLOCK, BLOCK)], adj_sem.at[k]
        )
        for k in range(slots)
    ]

    def exchange(t, j, owner):
        dx, dz = ORDER[j]
        return pltpu.make_async_remote_copy(
            src_ref=outgoing.at[t, j],
            dst_ref=tables[t].at[blocks + owner],
            send_sem=send_sem.at[t, j],
            recv_sem=recv_sem.at[t, j],
            device_id={"dom": at(dx, dz)},
            device_id_type=MESH,
        )

    def ship(t, g):
        rows = pl.ds(2 * g, 2)
        return pltpu.make_async_remote_copy(
            src_ref=result.at[t, rows],
            dst_ref=owns[t + 1].at[rows],
            send_sem=ship_send.at[t, g],
            recv_sem=ship_recv.at[t, g],
            device_id=along(1),
            device_id_type=MESH,
        )

    def leave(t, g):
        rows = pl.ds(2 * g, 2)
        return pltpu.make_async_copy(result.at[t, rows], out.at[t, rows], out_sem.at[t, g])

    def hand(n):
        source, target, by = ((0, 1, 1), (0, 2, 2), (1, 2, 1), (1, 3, 2), (2, 3, 1))[n]
        return pltpu.make_async_remote_copy(
            src_ref=held.at[source],
            dst_ref=held.at[target],
            send_sem=held_send.at[n],
            recv_sem=held_recv.at[target],
            device_id=along(by),
            device_id_type=MESH,
        )

    hands = (
        section < n_section - 1,
        (core == 0) & (section < n_section - 2),
        core == 0,
        (core == 0) & (section < n_section - 2),
        core == 0,
    )

    def own_to_table(t):
        return pltpu.make_async_copy(owns[t], tables[t].at[pl.ds(0, blocks)], own_sem.at[t])

    def send(t):
        if t == 0:
            load_x.wait()
        else:

            @pl.when(section == 0)
            def _():
                feed(t, 0, owns[t]).wait()

            @pl.when(section > 0)
            def _():
                for g in range(pairs):
                    ship(t - 1, g).wait_recv()

        own_to_table(t).start()
        for j, (dx, dz) in enumerate(ORDER):
            outgoing[t, j] = owns[t][send_list[part, at(dx, dz)]]
            if j:
                exchange(t, j - 1, part).start()
        tables[t][blocks + part] = owns[t][send_list[part, part]]
        exchange(t, PEERS - 1, part).start()

    def compute(t):
        if t > 0:

            @pl.when(section == 0)
            def _():
                feed(t, 1, held.at[t]).wait()

            @pl.when(section > 0)
            def _():
                hand((0, 0, 1, 3)[t]).wait_recv()

        for n in ((), (2, 3), (4,), ())[t]:

            @pl.when(hands[n])
            def _():
                hand(n).start()

        own_to_table(t).wait()
        for j, (dx, dz) in enumerate(ORDER):
            exchange(t, j, at(-dx, -dz)).wait_recv()
        beta = betas[section]

        def pair(g, carry):
            mixed = []
            for half in range(2):
                r = 2 * g + half
                total = None
                for k in range(slots // 2):
                    picked = jnp.concatenate(
                        [tables[t][col[r, 2 * k]], tables[t][col[r, 2 * k + 1]]], axis=0
                    )
                    term = jnp.dot(adjacency[r, k], picked, preferred_element_type=jnp.float32)
                    total = term if total is None else total + term
                anchor = held[t, r].astype(jnp.float32)
                mixed.append(((1.0 - TELEPORT) * total + TELEPORT * anchor).astype(jnp.bfloat16))
            mixture = jnp.concatenate(mixed, axis=0)
            product = jnp.dot(mixture, weight[...], preferred_element_type=jnp.float32)
            layer = (1.0 - beta) * mixture.astype(jnp.float32) + beta * product
            layer = jnp.maximum(layer, 0.0).astype(jnp.bfloat16)
            for half in range(2):
                result[t, 2 * g + half] = layer[half * BLOCK : (half + 1) * BLOCK]
            if t < STEPS - 1:

                @pl.when(section < n_section - 1)
                def _():
                    ship(t, g).start()

            leave(t, g).start()
            return carry

        lax.fori_loop(0, pairs, pair, 0)

    def on(which, *work):
        @pl.when(core == which)
        def _():
            for step, t in work:
                step(t)

    def pass_token(t):
        for j in range(PEERS):
            exchange(t, j, part).wait_send()
        pl.semaphore_signal(token, inc=1, device_id=along(1), device_id_type=MESH)

    def take_token(t):
        pl.semaphore_wait(token, 1)

    pl.semaphore_wait(barrier, PEERS + 4)
    on(0, (send, 0))

    for copy in load_adj:
        copy.start()
    load_held.wait()
    for n in (0, 1):

        @pl.when(hands[n])
        def _():
            hand(n).start()

    load_weight.wait()
    for copy in load_adj:
        copy.wait()

    def mask(r, carry):
        lane = lax.broadcasted_iota(jnp.int32, (BLOCK, 2 * BLOCK), 1)
        for k in range(slots // 2):
            live = lane < (counts[r] - 2 * k) * BLOCK
            adjacency[r, k] = jnp.where(live, adjacency[r, k], jnp.zeros((), jnp.bfloat16))
        return carry

    lax.fori_loop(0, blocks, mask, 0)

    on(0, (pass_token, 0), (compute, 0))
    on(1, (take_token, 0), (send, 0))
    send(1)
    on(0, (send, 2))
    on(1, (compute, 0))
    compute(1)
    on(0, (compute, 2))
    on(1, (send, 2))
    send(3)
    on(1, (compute, 2))
    compute(3)

    for t in range(STEPS):
        for g in range(pairs):
            leave(t, g).wait()
        if t:
            for j in range(PEERS):
                exchange(t, j, part).wait_send()

    @pl.when(core == 1)
    def _():
        for j in range(PEERS):
            exchange(0, j, part).wait_send()

    @pl.when(section < n_section - 1)
    def _():
        for t in range(STEPS - 1):
            for g in range(pairs):
                ship(t, g).wait_send()

    for n in range(len(hands)):

        @pl.when(hands[n])
        def _():
            hand(n).wait_send()


def solution(mesh):
    n_section, n_dom = mesh.shape["section"], mesh.shape["dom"]
    n_x = math.isqrt(n_dom)
    n_z = n_dom // n_x

    def body(carry_h, carry_h0, new_h0, weights, adj_blocks, col_index, counts, send_list):
        rows, width = carry_h.shape[1:]
        blocks, slots = adj_blocks.shape[:2]
        betas = jnp.asarray([math.log(1.0 + STRENGTH / (s + 1)) for s in range(n_section)], jnp.float32)
        tiles = (blocks, BLOCK, width)
        anywhere = pl.BlockSpec(memory_space=pl.ANY)
        scalars = pl.BlockSpec(memory_space=pltpu.SMEM)
        out = pl.pallas_call(
            functools.partial(kernel, n_section, n_x, n_z),
            out_shape=jax.ShapeDtypeStruct((STEPS, *tiles), jnp.bfloat16),
            in_specs=[scalars] * 4 + [anywhere] * 5,
            out_specs=anywhere,
            scratch_shapes=[pltpu.VMEM(tiles, jnp.bfloat16)] * STEPS
            + [pltpu.VMEM((blocks + n_dom, BLOCK, width), jnp.bfloat16)] * STEPS
            + [
                pltpu.VMEM((STEPS, PEERS, BLOCK, width), jnp.bfloat16),
                pltpu.VMEM((STEPS, *tiles), jnp.bfloat16),
                pltpu.VMEM((STEPS, *tiles), jnp.bfloat16),
                pltpu.VMEM((blocks, slots // 2, BLOCK, 2 * BLOCK), jnp.bfloat16),
                pltpu.VMEM((width, width), jnp.bfloat16),
                pltpu.SemaphoreType.REGULAR,
                pltpu.SemaphoreType.DMA((3,)),
                pltpu.SemaphoreType.DMA((2, STEPS)),
                pltpu.SemaphoreType.DMA((slots,)),
                pltpu.SemaphoreType.DMA((STEPS,)),
                pltpu.SemaphoreType.DMA((STEPS, PEERS)),
                pltpu.SemaphoreType.DMA((STEPS, PEERS)),
                pltpu.SemaphoreType.DMA((STEPS, blocks // 2)),
                pltpu.SemaphoreType.DMA((STEPS, blocks // 2)),
                pltpu.SemaphoreType.DMA((5,)),
                pltpu.SemaphoreType.DMA((STEPS,)),
                pltpu.SemaphoreType.DMA((STEPS, blocks // 2)),
            ],
            compiler_params=pltpu.CompilerParams(
                collective_id=0, has_side_effects=True, vmem_limit_bytes=62 << 20
            ),
        )(
            col_index, counts, send_list, betas,
            carry_h.reshape(1, *tiles), carry_h0.reshape(1, *tiles), new_h0.reshape(-1, *tiles), weights, adj_blocks,
        )
        return out.reshape(1, STEPS, rows, width)

    in_specs = (
        P("section", "dom", None),
        P("section", "dom", None),
        P(None, "dom", None),
        P("section", None, None),
        P("dom", None, None, None),
        P("dom", None),
        P("dom"),
        P(),
    )
    out_specs = P("section", None, "dom", None)
    return jax.shard_map(body, mesh=mesh, in_specs=in_specs, out_specs=out_specs, check_vma=False)
```

time: 347 us -> 150 us (0.43); the launches traced: 341 us -> 150 us
  waiting for transfers between devices: 148 us -> 0 us
  Pallas kernels: 0 us -> 145 us
  local copies, waits for them, and re-layouts: 61.3 us -> 4.47 us
  matrix products: 56.6 us -> 0 us
  other arithmetic: 40.9 us -> 0 us
  starting transfers between devices: 33.1 us -> 0 us
    pallas_call x0 -> x1, Pallas kernels: none -> 145 us  [body(): pl.pallas_call(functools.partial(kernel, n_section, n_x, n_z), out_shape=...]
    all_to_all x4 -> x0, waiting for transfers between devices: 106 us -> none  [body(): lax.all_to_all(outgoing, 'dom', split_axis=0, concat_axis=0, tiled=True)]
    gather x8 -> x0, local copies, waits for them, and re-layouts: 60.1 us -> none  [the longest x4 52.2 us: body(): picked = jnp.take(lookup, col_index, axis=0)]
    dot_general x8 -> x0, matrix products: 56.6 us -> none  [the longest x4 53.5 us: body(): jnp.einsum('rkij,rkjd->rid', masked_adj, picked, preferred_element_type=j...]
    ppermute x6 -> x0, waiting for transfers between devices: 42.6 us -> none  [shifted_2(): return lax.ppermute(value, axis, pairs)]
    all_to_all x4 -> x0, starting transfers between devices: 21.4 us -> none  [body(): lax.all_to_all(outgoing, 'dom', split_axis=0, concat_axis=0, tiled=True)]
    concatenate x4 -> x0, other arithmetic: 14.1 us -> none  [body(): lookup = jnp.concatenate([own_blocks, incoming], axis=0)]
    select_n x8 -> x0, other arithmetic: 13 us -> none  [the longest x4 11.1 us: body(): outgoing = jnp.take(own_blocks, outgoing_ids, axis=0)]
  transfers between devices with their start and end apart: 10 -> 0, of which waited for: 7 -> 0; matrix products, arithmetic and copies ran while one was open for 27% -> 0% of each run, Pallas kernels for 0% -> 0%
where the time goes in v1:
time: 150 us
  Pallas kernels  145 us (97%)
  local copies, waits for them, and re-layouts  4.47 us (3%)
    pallas_call x1, Pallas kernels, body(): pl.pallas_call(functools.partial(kernel, n_section, n_x, n_z), out_shape=...  145 us
    unnamed x1, local copies, waits for them, and re-layouts  4.47 us

profile of v1, /device:TPU:16, one launch (start us, length us, event | category | flops | bytes accessed | tf_op | source)
XLA Modules:
  0.0 149.9 jit_solution(8017774991693522583)
XLA Ops:
  0.0 145.4 %shard_map.91 = bf16[4,8,128,512]{3,2,1,0:T(8,128)(2,1)} custom-call(s32[8,24]{1,0:T(8,128)} %col.1, s32[8]{0:T(128)} %counts.1, s32[16,16]{1,0:T(8,128)} %send_list.1, f32[8]{0:T(128)} %constant.2.clone.betas, bf16[1,8,128,512]{3,2,1,0:T(8,128)(2,1)} %bitcast.6, bf16[1,8,128,512]{3,2,1,0:T(8,128)(2,1)} %bitcast.7, bf16[3,8,128,512]{3,2,1,0:T(8,128)(2,1)} %bitcast.5, ...), custom_call_target="tpu_custom_call" | custom-call | tf_op jit(solution)/shard_map/pallas_call | solution.py:292
  145.4 4.5 %copy.11 = bf16[1,4,1024,512]{3,2,1,0:T(8,128)(2,1)} copy(bf16[1,4,1024,512]{3,2,1,0:T(8,128)(2,1)} %bitcast.4) | data formatting | bytes 8388608

commit v2 on v1

v2 whole, which is shorter than its diff:
```python
import functools
import math

import jax
import jax.numpy as jnp
from jax import lax
from jax.experimental import pallas as pl
from jax.experimental.pallas import tpu as pltpu
from jax.sharding import PartitionSpec as P

BLOCK = 128
STEPS = 4
TELEPORT = 0.2
STRENGTH = 1.5
MESH = pl.DeviceIdType.MESH
HALVES = 2
CHUNKS = 4
PER = CHUNKS // HALVES

ORDER = (
    (1, 1), (-1, -1),
    (1, -1), (-1, 1),
    (1, 2), (-1, 0),
    (1, 0), (-1, 2),
    (2, 2),
    (2, 0), (0, 2),
    (2, 1), (0, -1),
    (2, -1), (0, 1),
)
PEERS = len(ORDER)
FIRST = 3


def kernel(n_section, n_x, n_z, col, counts, send_list, betas, carry_h, carry_h0, new_h0, weights, adj, out, *scratch):
    owns, scratch = [scratch[t * CHUNKS : (t + 1) * CHUNKS] for t in range(STEPS)], scratch[STEPS * CHUNKS :]
    tables, scratch = [scratch[t * HALVES : (t + 1) * HALVES] for t in range(STEPS)], scratch[STEPS * HALVES :]
    (
        outgoing, held, mixed, result, adjacency, weight,
        token, load_sem, feed_sem, adj_sem, own_sem, send_sem, recv_sem, ship_send, ship_recv, held_send, held_recv,
    ) = scratch
    section = lax.axis_index("section")
    part = lax.axis_index("dom")
    z, x = part // n_x, part % n_x
    core = section % 2
    blocks = held.shape[1]
    slots = adj.shape[1]
    wide = weight.shape[1] // CHUNKS
    half_wide = weight.shape[1] // HALVES

    def at(dx, dz):
        return ((z + dz + n_z) % n_z) * n_x + (x + dx + n_x) % n_x

    def along(by):
        return {"section": (section + by + n_section) % n_section}

    barrier = pltpu.get_barrier_semaphore()
    for dx, dz in ORDER:
        pl.semaphore_signal(barrier, inc=1, device_id={"dom": at(dx, dz)}, device_id_type=MESH)
    for by in (1, -1, 2, -2):
        pl.semaphore_signal(barrier, inc=1, device_id=along(by), device_id_type=MESH)

    def columns(c):
        return pl.ds(c * wide, wide)

    def load_x(c):
        return pltpu.make_async_copy(carry_h.at[0, :, :, columns(c)], owns[0][c], load_sem.at[0])

    load_held = pltpu.make_async_copy(carry_h0.at[0], held.at[0], load_sem.at[1])
    load_weight = pltpu.make_async_copy(weights.at[0], weight, load_sem.at[2])
    for c in range(CHUNKS):
        load_x(c).start()
    load_held.start()
    load_weight.start()

    def feed_x(t, c):
        return pltpu.make_async_copy(new_h0.at[t - 1, :, :, columns(c)], owns[t][c], feed_sem.at[0, t - 1])

    def feed_held(t):
        return pltpu.make_async_copy(new_h0.at[t - 1], held.at[t], feed_sem.at[1, t - 1])

    @pl.when(section == 0)
    def _():
        for t in range(1, STEPS):
            for c in range(CHUNKS):
                feed_x(t, c).start()
            feed_held(t).start()

    load_adj = [
        pltpu.make_async_copy(
            adj.at[:, k], adjacency.at[:, k // 2, :, pl.ds((k % 2) * BLOCK, BLOCK)], adj_sem
        )
        for k in range(slots)
    ]

    def exchange(t, c, j, owner):
        dx, dz = ORDER[j]
        return pltpu.make_async_remote_copy(
            src_ref=outgoing.at[t, c, j],
            dst_ref=tables[t][c // PER].at[c % PER, blocks + owner],
            send_sem=send_sem.at[STEPS if t == 0 and c >= FIRST else t],
            recv_sem=recv_sem.at[t, c // PER],
            device_id={"dom": at(dx, dz)},
            device_id_type=MESH,
        )

    def sent(n, first, count):
        part_of = outgoing.at[n % STEPS, pl.ds(first, count)]
        return pltpu.make_async_copy(part_of, part_of, send_sem.at[n])

    def arrived(t, h):
        part_of = tables[t][h].at[:, pl.ds(blocks, PEERS)]
        return pltpu.make_async_copy(part_of, part_of, recv_sem.at[t, h])

    def own_done(t, h):
        part_of = tables[t][h].at[:, pl.ds(0, blocks)]
        return pltpu.make_async_copy(part_of, part_of, own_sem.at[t, h])

    def ship(t, c):
        return pltpu.make_async_remote_copy(
            src_ref=result.at[t, c],
            dst_ref=owns[t + 1][c],
            send_sem=ship_send.at[t],
            recv_sem=ship_recv.at[t, c],
            device_id=along(1),
            device_id_type=MESH,
        )

    def hand(n):
        source, target, by = ((0, 1, 1), (0, 2, 2), (1, 2, 1), (1, 3, 2), (2, 3, 1))[n]
        return pltpu.make_async_remote_copy(
            src_ref=held.at[source],
            dst_ref=held.at[target],
            send_sem=held_send.at[n],
            recv_sem=held_recv.at[target],
            device_id=along(by),
            device_id_type=MESH,
        )

    hands = (
        section < n_section - 1,
        (core == 0) & (section < n_section - 2),
        core == 0,
        (core == 0) & (section < n_section - 2),
        core == 0,
    )

    def hand_on(n):
        @pl.when(hands[n])
        def _():
            hand(n).start()

    def own_to_table(t, c):
        return pltpu.make_async_copy(
            owns[t][c], tables[t][c // PER].at[c % PER, pl.ds(0, blocks)], own_sem.at[t, c // PER]
        )

    def send(t):
        if t == 0:
            pltpu.make_async_copy(held.at[0], held.at[0], load_sem.at[0]).wait()
        else:

            @pl.when(section == 0)
            def _():
                pltpu.make_async_copy(held.at[t], held.at[t], feed_sem.at[0, t - 1]).wait()

        for c in range(CHUNKS):
            if t:

                @pl.when(section > 0)
                def _():
                    ship(t - 1, c).wait_recv()

            own_to_table(t, c).start()
            for j, (dx, dz) in enumerate(ORDER):
                outgoing[t, c, j] = owns[t][c][send_list[part, at(dx, dz)]]
                if j:
                    exchange(t, c, j - 1, part).start()
            tables[t][c // PER][c % PER, blocks + part] = owns[t][c][send_list[part, part]]
            exchange(t, c, PEERS - 1, part).start()

    def wait_held(t):
        if t == 0:
            load_held.wait()
        else:

            @pl.when(section == 0)
            def _():
                feed_held(t).wait()

            @pl.when(section > 0)
            def _():
                hand((0, 0, 1, 3)[t]).wait_recv()

    def wait_table(t, h):
        own_done(t, h).wait()
        arrived(t, h).wait()

    def aggregate(t, h):
        table = tables[t][h]
        lanes = slice(h * half_wide, (h + 1) * half_wide)

        def entry(n):
            return jnp.concatenate([table[c, n] for c in range(PER)], axis=1)

        def rows(g, carry):
            for i in range(2):
                r = 2 * g + i
                total = None
                for k in range(slots // 2):
                    picked = jnp.concatenate([entry(col[r, 2 * k]), entry(col[r, 2 * k + 1])], axis=0)
                    term = jnp.dot(adjacency[r, k], picked, preferred_element_type=jnp.float32)
                    total = term if total is None else total + term
                anchor = held[t, r, :, lanes].astype(jnp.float32)
                mixed[r, :, lanes] = ((1.0 - TELEPORT) * total + TELEPORT * anchor).astype(jnp.bfloat16)
            return carry

        lax.fori_loop(0, blocks // 2, rows, 0)

    def finish(t):
        beta = betas[section]
        for h in range(HALVES):
            lanes = slice(h * half_wide, (h + 1) * half_wide)

            def rows(g, carry):
                mixture = jnp.concatenate([mixed[2 * g], mixed[2 * g + 1]], axis=0)
                product = jnp.dot(mixture, weight[:, lanes], preferred_element_type=jnp.float32)
                layer = (1.0 - beta) * mixture[:, lanes].astype(jnp.float32) + beta * product
                layer = jnp.maximum(layer, 0.0).astype(jnp.bfloat16)
                for i in range(2):
                    rows_of = layer[i * BLOCK : (i + 1) * BLOCK]
                    out[t, 2 * g + i, :, lanes] = rows_of
                    if t < STEPS - 1:
                        for c in range(PER):
                            result[t, h * PER + c, 2 * g + i] = rows_of[:, c * wide : (c + 1) * wide]
                return carry

            lax.fori_loop(0, blocks // 2, rows, 0)
            if t < STEPS - 1:

                @pl.when(section < n_section - 1)
                def _():
                    for c in range(h * PER, (h + 1) * PER):
                        ship(t, c).start()

    def let_in(n):
        @pl.when(section == 1)
        def _():
            pl.semaphore_signal(token.at[n], inc=1, device_id=along(-1), device_id_type=MESH)

    def first_half(t):
        if t:
            wait_held(t)
        wait_table(t, 0)
        if t == 1:
            let_in(1)
        aggregate(t, 0)

    def second_half(t):
        wait_table(t, 1)
        if t == 2:
            let_in(2)
        aggregate(t, 1)
        finish(t)

    def on(which, *work):
        @pl.when(core == which)
        def _():
            for step, t in work:
                step(t)

    def hold_back(n):
        @pl.when(section == 0)
        def _():
            pl.semaphore_wait(token.at[n], 1)

    def give_way(t):
        sent(0, 0, FIRST).wait()
        pl.semaphore_signal(token.at[0], inc=1, device_id=along(1), device_id_type=MESH)

    def take_turn(t):
        pl.semaphore_wait(token.at[0], 1)

    pl.semaphore_wait(barrier, PEERS + 4)
    on(0, (send, 0))

    for copy in load_adj:
        copy.start()
    load_held.wait()
    hand_on(0)
    load_weight.wait()
    pltpu.make_async_copy(adjacency, adjacency, adj_sem).wait()

    def mask(r, carry):
        lane = lax.broadcasted_iota(jnp.int32, (BLOCK, 2 * BLOCK), 1)
        for k in range(slots // 2):
            live = lane < (counts[r] - 2 * k) * BLOCK
            adjacency[r, k] = jnp.where(live, adjacency[r, k], jnp.zeros((), jnp.bfloat16))
        return carry

    lax.fori_loop(0, blocks, mask, 0)

    on(0, (give_way, 0))
    on(1, (take_turn, 0), (send, 0))
    on(1, (send, 1))
    first_half(0)
    hand_on(1)
    second_half(0)
    on(0, (hold_back, 1), (send, 1))

    @pl.when(section == 0)
    def _():
        send(2)

    first_half(1)
    hand_on(2)

    @pl.when((core == 0) & (section > 0))
    def _():
        send(2)

    second_half(1)
    hand_on(3)
    on(1, (send, 2), (send, 3))
    first_half(2)
    hand_on(4)
    second_half(2)
    on(0, (hold_back, 2), (send, 3))
    first_half(3)
    second_half(3)

    @pl.when(core == 1)
    def _():
        sent(0, 0, FIRST).wait()

    sent(STEPS, FIRST, CHUNKS - FIRST).wait()
    for t in range(1, STEPS):
        sent(t, 0, CHUNKS).wait()

    @pl.when(section < n_section - 1)
    def _():
        for t in range(STEPS - 1):
            pltpu.make_async_copy(result.at[t], result.at[t], ship_send.at[t]).wait()

    for n in range(len(hands)):

        @pl.when(hands[n])
        def _():
            hand(n).wait_send()


def solution(mesh):
    n_section, n_dom = mesh.shape["section"], mesh.shape["dom"]
    n_x = math.isqrt(n_dom)
    n_z = n_dom // n_x

    def body(carry_h, carry_h0, new_h0, weights, adj_blocks, col_index, counts, send_list):
        rows, width = carry_h.shape[1:]
        blocks, slots = adj_blocks.shape[:2]
        wide = width // CHUNKS
        betas = jnp.asarray([math.log(1.0 + STRENGTH / (s + 1)) for s in range(n_section)], jnp.float32)
        tiles = (blocks, BLOCK, width)
        anywhere = pl.BlockSpec(memory_space=pltpu.HBM)
        scalars = pl.BlockSpec(memory_space=pltpu.SMEM)
        vmem = lambda *shape: pltpu.VMEM(shape, jnp.bfloat16)
        dma = lambda *shape: pltpu.SemaphoreType.DMA(shape)
        out = pl.pallas_call(
            functools.partial(kernel, n_section, n_x, n_z),
            out_shape=vmem(STEPS, *tiles),
            in_specs=[scalars] * 4 + [anywhere] * 5,
            out_specs=pl.BlockSpec(memory_space=pltpu.VMEM),
            scratch_shapes=[vmem(blocks, BLOCK, wide)] * (STEPS * CHUNKS)
            + [vmem(PER, blocks + n_dom, BLOCK, wide)] * (STEPS * HALVES)
            + [
                vmem(STEPS, CHUNKS, PEERS, BLOCK, wide),
                vmem(STEPS, *tiles),
                vmem(*tiles),
                vmem(STEPS - 1, CHUNKS, blocks, BLOCK, wide),
                vmem(blocks, slots // 2, BLOCK, 2 * BLOCK),
                vmem(width, width),
                pltpu.SemaphoreType.REGULAR((3,)),
                dma(3),
                dma(2, STEPS - 1),
                pltpu.SemaphoreType.DMA,
                dma(STEPS, HALVES),
                dma(STEPS + 1),
                dma(STEPS, HALVES),
                dma(STEPS - 1),
                dma(STEPS - 1, CHUNKS),
                dma(5),
                dma(STEPS),
            ],
            compiler_params=pltpu.CompilerParams(
                collective_id=0, has_side_effects=True, vmem_limit_bytes=67_043_328 - (4 << 20) - (64 << 10)
            ),
        )(
            col_index, counts, send_list, betas,
            carry_h.reshape(1, *tiles), carry_h0.reshape(1, *tiles), new_h0.reshape(-1, *tiles), weights, adj_blocks,
        )
        return out.reshape(1, STEPS, rows, width)

    in_specs = (
        P("section", "dom", None),
        P("section", "dom", None),
        P(None, "dom", None),
        P("section", None, None),
        P("dom", None, None, None),
        P("dom", None),
        P("dom"),
        P(),
    )
    out_specs = P("section", None, "dom", None)
    return jax.shard_map(body, mesh=mesh, in_specs=in_specs, out_specs=out_specs, check_vma=False)
```

time: 150 us -> 113 us (0.75)
  Pallas kernels: 145 us -> 110 us
  local copies, waits for them, and re-layouts: 4.47 us -> 2.02 us
    pallas_call x1, Pallas kernels: 145 us -> 110 us  [body(): pl.pallas_call(functools.partial(kernel, n_section, n_x, n_z), out_shape=...]
    unnamed x1, local copies, waits for them, and re-layouts: 4.47 us -> 2.02 us
where the time goes in v2:
time: 113 us; the launch traced here: 112 us
  Pallas kernels  110 us (97%)
  local copies, waits for them, and re-layouts  2.02 us (2%)
    pallas_call x1, Pallas kernels, body(): pl.pallas_call(functools.partial(kernel, n_section, n_x, n_z), out_shape=...  110 us

profile of v2, /device:TPU:16, one launch (start us, length us, event | category | flops | bytes accessed | tf_op | source)
XLA Modules:
  0.0 112.4 jit_solution(1687315591601995273)
XLA Ops:
  0.0 110.4 %shard_map.91 = bf16[4,8,128,512]{3,2,1,0:T(8,128)(2,1)S(1)} custom-call(s32[8,24]{1,0:T(8,128)} %col.1, s32[8]{0:T(128)} %counts.1, s32[16,16]{1,0:T(8,128)} %send_list.1, f32[8]{0:T(128)} %constant.2.clone.betas, bf16[1,8,128,512]{3,2,1,0:T(8,128)(2,1)} %bitcast.6, bf16[1,8,128,512]{3,2,1,0:T(8,128)(2,1)} %bitcast.7, bf16[3,8,128,512]{3,2,1,0:T(8,128)(2,1)} %bitcast.5, ...), custom_call_target="tpu_custom_call" | custom-call | tf_op jit(solution)/shard_map/pallas_call | solution.py:366
  110.4 2.0 %copy.11 = bf16[1,4,1024,512]{3,2,1,0:T(8,128)(2,1)} copy(bf16[1,4,1024,512]{3,2,1,0:T(8,128)(2,1)S(1)} %bitcast.4) | data formatting | bytes 8388608

commit v3 on v2

--- a/solution.py
+++ b/solution.py
@@ -13,19 +13,19 @@
 TELEPORT = 0.2
 STRENGTH = 1.5
 MESH = pl.DeviceIdType.MESH
+CHUNKS = 4
 HALVES = 2
-CHUNKS = 4
 PER = CHUNKS // HALVES
 
 ORDER = (
+    (2, 2),
+    (2, 1), (0, -1),
+    (2, -1), (0, 1),
+    (1, 2), (-1, 0),
+    (1, 0), (-1, 2),
     (1, 1), (-1, -1),
     (1, -1), (-1, 1),
-    (1, 2), (-1, 0),
-    (1, 0), (-1, 2),
-    (2, 2),
     (2, 0), (0, 2),
-    (2, 1), (0, -1),
-    (2, -1), (0, 1),
 )
 PEERS = len(ORDER)
 FIRST = 3
@@ -35,7 +35,7 @@
     owns, scratch = [scratch[t * CHUNKS : (t + 1) * CHUNKS] for t in range(STEPS)], scratch[STEPS * CHUNKS :]
     tables, scratch = [scratch[t * HALVES : (t + 1) * HALVES] for t in range(STEPS)], scratch[STEPS * HALVES :]
     (
-        outgoing, held, mixed, result, adjacency, weight,
+        outgoing, held, partial, result, adjacency, weight,
         token, load_sem, feed_sem, adj_sem, own_sem, send_sem, recv_sem, ship_send, ship_recv, held_send, held_recv,
     ) = scratch
     section = lax.axis_index("section")
@@ -45,7 +45,7 @@
     blocks = held.shape[1]
     slots = adj.shape[1]
     wide = weight.shape[1] // CHUNKS
-    half_wide = weight.shape[1] // HALVES
+    half = PER * wide
 
     def at(dx, dz):
         return ((z + dz + n_z) % n_z) * n_x + (x + dx + n_x) % n_x
@@ -115,10 +115,11 @@
         part_of = tables[t][h].at[:, pl.ds(0, blocks)]
         return pltpu.make_async_copy(part_of, part_of, own_sem.at[t, h])
 
-    def ship(t, c):
+    def ship(t, c, first, count):
+        rows = pl.ds(first, count)
         return pltpu.make_async_remote_copy(
-            src_ref=result.at[t, c],
-            dst_ref=owns[t + 1][c],
+            src_ref=result.at[t, c, rows],
+            dst_ref=owns[t + 1][c].at[rows],
             send_sem=ship_send.at[t],
             recv_sem=ship_recv.at[t, c],
             device_id=along(1),
@@ -154,8 +155,10 @@
             owns[t][c], tables[t][c // PER].at[c % PER, pl.ds(0, blocks)], own_sem.at[t, c // PER]
         )
 
-    def send(t):
-        if t == 0:
+    def send(t, chunks=range(CHUNKS)):
+        if 0 not in chunks:
+            pass
+        elif t == 0:
             pltpu.make_async_copy(held.at[0], held.at[0], load_sem.at[0]).wait()
         else:
 
@@ -163,12 +166,12 @@
             def _():
                 pltpu.make_async_copy(held.at[t], held.at[t], feed_sem.at[0, t - 1]).wait()
 
-        for c in range(CHUNKS):
+        for c in chunks:
             if t:
 
                 @pl.when(section > 0)
                 def _():
-                    ship(t - 1, c).wait_recv()
+                    ship(t - 1, c, 0, blocks).wait_recv()
 
             own_to_table(t, c).start()
             for j, (dx, dz) in enumerate(ORDER):
@@ -195,52 +198,63 @@
         own_done(t, h).wait()
         arrived(t, h).wait()
 
-    def aggregate(t, h):
+    def mix(t, h, r):
         table = tables[t][h]
-        lanes = slice(h * half_wide, (h + 1) * half_wide)
 
         def entry(n):
             return jnp.concatenate([table[c, n] for c in range(PER)], axis=1)
 
+        total = None
+        for k in range(slots // 2):
+            picked = jnp.concatenate([entry(col[r, 2 * k]), entry(col[r, 2 * k + 1])], axis=0)
+            term = jnp.dot(adjacency[r, k], picked, preferred_element_type=jnp.float32)
+            total = term if total is None else total + term
+        anchor = held[t, r, :, h * half : (h + 1) * half].astype(jnp.float32)
+        return ((1.0 - TELEPORT) * total + TELEPORT * anchor).astype(jnp.bfloat16)
+
+    def begin(t):
+        beta = betas[section]
+
         def rows(g, carry):
-            for i in range(2):
-                r = 2 * g + i
-                total = None
-                for k in range(slots // 2):
-                    picked = jnp.concatenate([entry(col[r, 2 * k]), entry(col[r, 2 * k + 1])], axis=0)
-                    term = jnp.dot(adjacency[r, k], picked, preferred_element_type=jnp.float32)
-                    total = term if total is None else total + term
-                anchor = held[t, r, :, lanes].astype(jnp.float32)
-                mixed[r, :, lanes] = ((1.0 - TELEPORT) * total + TELEPORT * anchor).astype(jnp.bfloat16)
+            left = jnp.concatenate([mix(t, 0, 2 * g), mix(t, 0, 2 * g + 1)], axis=0)
+            product = beta * jnp.dot(left, weight[:half], preferred_element_type=jnp.float32)
+            partial[g, :, :half] = product[:, :half] + (1.0 - beta) * left.astype(jnp.float32)
+            partial[g, :, half:] = product[:, half:]
             return carry
 
         lax.fori_loop(0, blocks // 2, rows, 0)
 
     def finish(t):
         beta = betas[section]
-        for h in range(HALVES):
-            lanes = slice(h * half_wide, (h + 1) * half_wide)
-
-            def rows(g, carry):
-                mixture = jnp.concatenate([mixed[2 * g], mixed[2 * g + 1]], axis=0)
-                product = jnp.dot(mixture, weight[:, lanes], preferred_element_type=jnp.float32)
-                layer = (1.0 - beta) * mixture[:, lanes].astype(jnp.float32) + beta * product
-                layer = jnp.maximum(layer, 0.0).astype(jnp.bfloat16)
-                for i in range(2):
-                    rows_of = layer[i * BLOCK : (i + 1) * BLOCK]
-                    out[t, 2 * g + i, :, lanes] = rows_of
-                    if t < STEPS - 1:
-                        for c in range(PER):
-                            result[t, h * PER + c, 2 * g + i] = rows_of[:, c * wide : (c + 1) * wide]
-                return carry
-
-            lax.fori_loop(0, blocks // 2, rows, 0)
+
+        def rows(g, carry):
+            right = jnp.concatenate([mix(t, 1, 2 * g), mix(t, 1, 2 * g + 1)], axis=0)
+            layer = partial[g] + beta * jnp.dot(right, weight[half:], preferred_element_type=jnp.float32)
+            layer = jnp.concatenate(
+                [layer[:, :half], layer[:, half:] + (1.0 - beta) * right.astype(jnp.float32)], axis=1
+            )
+            layer = jnp.maximum(layer, 0.0).astype(jnp.bfloat16)
+            for i in range(2):
+                rows_of = layer[i * BLOCK : (i + 1) * BLOCK]
+                out[t, 2 * g + i] = rows_of
+                if t < STEPS - 1:
+                    for c in range(CHUNKS):
+                        result[t, c, 2 * g + i] = rows_of[:, c * wide : (c + 1) * wide]
             if t < STEPS - 1:
 
                 @pl.when(section < n_section - 1)
                 def _():
-                    for c in range(h * PER, (h + 1) * PER):
-                        ship(t, c).start()
+                    ship(t, 0, 2 * g, 2).start()
+
+            return carry
+
+        lax.fori_loop(0, blocks // 2, rows, 0)
+        if t < STEPS - 1:
+
+            @pl.when(section < n_section - 1)
+            def _():
+                for c in range(1, CHUNKS):
+                    ship(t, c, 0, blocks).start()
 
     def let_in(n):
         @pl.when(section == 1)
@@ -253,13 +267,12 @@
         wait_table(t, 0)
         if t == 1:
             let_in(1)
-        aggregate(t, 0)
+        begin(t)
 
     def second_half(t):
         wait_table(t, 1)
         if t == 2:
             let_in(2)
-        aggregate(t, 1)
         finish(t)
 
     def on(which, *work):
@@ -316,9 +329,14 @@
 
     @pl.when((core == 0) & (section > 0))
     def _():
-        send(2)
+        send(2, (0, 1, 2))
 
     second_half(1)
+
+    @pl.when((core == 0) & (section > 0))
+    def _():
+        send(2, (3,))
+
     hand_on(3)
     on(1, (send, 2), (send, 3))
     first_half(2)
@@ -373,7 +391,7 @@
             + [
                 vmem(STEPS, CHUNKS, PEERS, BLOCK, wide),
                 vmem(STEPS, *tiles),
-                vmem(*tiles),
+                pltpu.VMEM((blocks // 2, 2 * BLOCK, width), jnp.float32),
                 vmem(STEPS - 1, CHUNKS, blocks, BLOCK, wide),
                 vmem(blocks, slots // 2, BLOCK, 2 * BLOCK),
                 vmem(width, width),

time: 113 us -> 109 us (0.965)
  Pallas kernels: 110 us -> 107 us
    pallas_call x1, Pallas kernels: 110 us -> 107 us  [body(): pl.pallas_call(functools.partial(kernel, n_section, n_x, n_z), out_shape=...]
where the time goes in v3:
time: 109 us
  Pallas kernels  107 us (98%)
  local copies, waits for them, and re-layouts  2.02 us (2%)
    pallas_call x1, Pallas kernels, body(): pl.pallas_call(functools.partial(kernel, n_section, n_x, n_z), out_shape=...  107 us

profile of v3, /device:TPU:16, one launch (start us, length us, event | category | flops | bytes accessed | tf_op | source)
XLA Modules:
  0.0 108.9 jit_solution(2582106440262885281)
XLA Ops:
  0.0 106.9 %shard_map.91 = bf16[4,8,128,512]{3,2,1,0:T(8,128)(2,1)S(1)} custom-call(s32[8,24]{1,0:T(8,128)} %col.1, s32[8]{0:T(128)} %counts.1, s32[16,16]{1,0:T(8,128)} %send_list.1, f32[8]{0:T(128)} %constant.2.clone.betas, bf16[1,8,128,512]{3,2,1,0:T(8,128)(2,1)} %bitcast.6, bf16[1,8,128,512]{3,2,1,0:T(8,128)(2,1)} %bitcast.7, bf16[3,8,128,512]{3,2,1,0:T(8,128)(2,1)} %bitcast.5, ...), custom_call_target="tpu_custom_call" | custom-call | tf_op jit(solution)/shard_map/pallas_call | solution.py:384
  106.9 2.0 %copy.11 = bf16[1,4,1024,512]{3,2,1,0:T(8,128)(2,1)} copy(bf16[1,4,1024,512]{3,2,1,0:T(8,128)(2,1)S(1)} %bitcast.4) | data formatting | bytes 8388608

commit v4 on v3

--- a/solution.py
+++ b/solution.py
@@ -19,23 +19,25 @@
 
 ORDER = (
     (2, 2),
-    (2, 1), (0, -1),
-    (2, -1), (0, 1),
-    (1, 2), (-1, 0),
-    (1, 0), (-1, 2),
+    (2, 1), (1, 2), (2, -1), (-1, 2),
     (1, 1), (-1, -1),
     (1, -1), (-1, 1),
     (2, 0), (0, 2),
+    (1, 0), (-1, 0), (0, 1), (0, -1),
 )
 PEERS = len(ORDER)
 FIRST = 3
 
 
-def kernel(n_section, n_x, n_z, col, counts, send_list, betas, carry_h, carry_h0, new_h0, weights, adj, out, *scratch):
+def beta_at(layer):
+    return math.log(1.0 + STRENGTH / (layer + 1))
+
+
+def kernel(n_section, n_x, n_z, col, counts, send_list, carry_h, carry_h0, new_h0, weights, adj, out, *scratch):
     owns, scratch = [scratch[t * CHUNKS : (t + 1) * CHUNKS] for t in range(STEPS)], scratch[STEPS * CHUNKS :]
     tables, scratch = [scratch[t * HALVES : (t + 1) * HALVES] for t in range(STEPS)], scratch[STEPS * HALVES :]
     (
-        outgoing, held, partial, result, adjacency, weight,
+        outgoing, held, partial, lines, result, adjacency, weight,
         token, load_sem, feed_sem, adj_sem, own_sem, send_sem, recv_sem, ship_send, ship_recv, held_send, held_recv,
     ) = scratch
     section = lax.axis_index("section")
@@ -97,15 +99,15 @@
         return pltpu.make_async_remote_copy(
             src_ref=outgoing.at[t, c, j],
             dst_ref=tables[t][c // PER].at[c % PER, blocks + owner],
-            send_sem=send_sem.at[STEPS if t == 0 and c >= FIRST else t],
+            send_sem=send_sem.at[t, int(c >= FIRST)],
             recv_sem=recv_sem.at[t, c // PER],
             device_id={"dom": at(dx, dz)},
             device_id_type=MESH,
         )
 
-    def sent(n, first, count):
-        part_of = outgoing.at[n % STEPS, pl.ds(first, count)]
-        return pltpu.make_async_copy(part_of, part_of, send_sem.at[n])
+    def sent(t, late):
+        part_of = outgoing.at[t, pl.ds(FIRST, CHUNKS - FIRST) if late else pl.ds(0, FIRST)]
+        return pltpu.make_async_copy(part_of, part_of, send_sem.at[t, late])
 
     def arrived(t, h):
         part_of = tables[t][h].at[:, pl.ds(blocks, PEERS)]
@@ -198,6 +200,12 @@
         own_done(t, h).wait()
         arrived(t, h).wait()
 
+    def beta_of():
+        value = jnp.float32(beta_at(n_section - 1))
+        for s in range(n_section - 1):
+            value = jnp.where(section == s, jnp.float32(beta_at(s)), value)
+        return value
+
     def mix(t, h, r):
         table = tables[t][h]
 
@@ -212,23 +220,35 @@
         anchor = held[t, r, :, h * half : (h + 1) * half].astype(jnp.float32)
         return ((1.0 - TELEPORT) * total + TELEPORT * anchor).astype(jnp.bfloat16)
 
+    def pipelined(t, h, use, after=lambda g: None):
+        def gather(g):
+            lines[g] = jnp.concatenate([mix(t, h, 2 * g), mix(t, h, 2 * g + 1)], axis=0)
+
+        def rows(g, carry):
+            use(g - 1, lines[g - 1])
+            gather(g)
+            after(g - 1)
+            return carry
+
+        gather(0)
+        lax.fori_loop(1, blocks // 2, rows, 0)
+        use(blocks // 2 - 1, lines[blocks // 2 - 1])
+        after(blocks // 2 - 1)
+
     def begin(t):
-        beta = betas[section]
-
-        def rows(g, carry):
-            left = jnp.concatenate([mix(t, 0, 2 * g), mix(t, 0, 2 * g + 1)], axis=0)
+        beta = beta_of()
+
+        def use(g, left):
             product = beta * jnp.dot(left, weight[:half], preferred_element_type=jnp.float32)
             partial[g, :, :half] = product[:, :half] + (1.0 - beta) * left.astype(jnp.float32)
             partial[g, :, half:] = product[:, half:]
-            return carry
-
-        lax.fori_loop(0, blocks // 2, rows, 0)
+
+        pipelined(t, 0, use)
 
     def finish(t):
-        beta = betas[section]
-
-        def rows(g, carry):
-            right = jnp.concatenate([mix(t, 1, 2 * g), mix(t, 1, 2 * g + 1)], axis=0)
+        beta = beta_of()
+
+        def use(g, right):
             layer = partial[g] + beta * jnp.dot(right, weight[half:], preferred_element_type=jnp.float32)
             layer = jnp.concatenate(
                 [layer[:, :half], layer[:, half:] + (1.0 - beta) * right.astype(jnp.float32)], axis=1
@@ -240,15 +260,15 @@
                 if t < STEPS - 1:
                     for c in range(CHUNKS):
                         result[t, c, 2 * g + i] = rows_of[:, c * wide : (c + 1) * wide]
+
+        def after(g):
             if t < STEPS - 1:
 
                 @pl.when(section < n_section - 1)
                 def _():
                     ship(t, 0, 2 * g, 2).start()
 
-            return carry
-
-        lax.fori_loop(0, blocks // 2, rows, 0)
+        pipelined(t, 1, use, after)
         if t < STEPS - 1:
 
             @pl.when(section < n_section - 1)
@@ -287,7 +307,7 @@
             pl.semaphore_wait(token.at[n], 1)
 
     def give_way(t):
-        sent(0, 0, FIRST).wait()
+        sent(0, 0).wait()
         pl.semaphore_signal(token.at[0], inc=1, device_id=along(1), device_id_type=MESH)
 
     def take_turn(t):
@@ -348,11 +368,10 @@
 
     @pl.when(core == 1)
     def _():
-        sent(0, 0, FIRST).wait()
-
-    sent(STEPS, FIRST, CHUNKS - FIRST).wait()
-    for t in range(1, STEPS):
-        sent(t, 0, CHUNKS).wait()
+        sent(0, 0).wait()
+
+    for t, late in ((0, 1), (1, 0), (1, 1), (2, 0), (2, 1), (3, 0), (3, 1)):
+        sent(t, late).wait()
 
     @pl.when(section < n_section - 1)
     def _():
@@ -375,7 +394,6 @@
         rows, width = carry_h.shape[1:]
         blocks, slots = adj_blocks.shape[:2]
         wide = width // CHUNKS
-        betas = jnp.asarray([math.log(1.0 + STRENGTH / (s + 1)) for s in range(n_section)], jnp.float32)
         tiles = (blocks, BLOCK, width)
         anywhere = pl.BlockSpec(memory_space=pltpu.HBM)
         scalars = pl.BlockSpec(memory_space=pltpu.SMEM)
@@ -384,7 +402,7 @@
         out = pl.pallas_call(
             functools.partial(kernel, n_section, n_x, n_z),
             out_shape=vmem(STEPS, *tiles),
-            in_specs=[scalars] * 4 + [anywhere] * 5,
+            in_specs=[scalars] * 3 + [anywhere] * 5,
             out_specs=pl.BlockSpec(memory_space=pltpu.VMEM),
             scratch_shapes=[vmem(blocks, BLOCK, wide)] * (STEPS * CHUNKS)
             + [vmem(PER, blocks + n_dom, BLOCK, wide)] * (STEPS * HALVES)
@@ -392,6 +410,7 @@
                 vmem(STEPS, CHUNKS, PEERS, BLOCK, wide),
                 vmem(STEPS, *tiles),
                 pltpu.VMEM((blocks // 2, 2 * BLOCK, width), jnp.float32),
+                vmem(blocks // 2, 2 * BLOCK, width // HALVES),
                 vmem(STEPS - 1, CHUNKS, blocks, BLOCK, wide),
                 vmem(blocks, slots // 2, BLOCK, 2 * BLOCK),
                 vmem(width, width),
@@ -400,7 +419,7 @@
                 dma(2, STEPS - 1),
                 pltpu.SemaphoreType.DMA,
                 dma(STEPS, HALVES),
-                dma(STEPS + 1),
+                dma(STEPS, 2),
                 dma(STEPS, HALVES),
                 dma(STEPS - 1),
                 dma(STEPS - 1, CHUNKS),
@@ -411,7 +430,7 @@
                 collective_id=0, has_side_effects=True, vmem_limit_bytes=67_043_328 - (4 << 20) - (64 << 10)
             ),
         )(
-            col_index, counts, send_list, betas,
+            col_index, counts, send_list,
             carry_h.reshape(1, *tiles), carry_h0.reshape(1, *tiles), new_h0.reshape(-1, *tiles), weights, adj_blocks,
         )
         return out.reshape(1, STEPS, rows, width)

time: 109 us -> 108 us (level)
    pallas_call x1, Pallas kernels: 107 us -> 106 us  [body(): pl.pallas_call(functools.partial(kernel, n_section, n_x, n_z), out_shape=...]
where the time goes in v4:
time: 108 us
  Pallas kernels  106 us (98%)
  local copies, waits for them, and re-layouts  2.02 us (2%)
    pallas_call x1, Pallas kernels, body(): pl.pallas_call(functools.partial(kernel, n_section, n_x, n_z), out_shape=...  106 us

profile of v4, /device:TPU:16, one launch (start us, length us, event | category | flops | bytes accessed | tf_op | source)
XLA Modules:
  0.0 107.7 jit_solution(11197283139933589909)
XLA Ops:
  0.0 105.7 %shard_map.82 = bf16[4,8,128,512]{3,2,1,0:T(8,128)(2,1)S(1)} custom-call(s32[8,24]{1,0:T(8,128)} %col.1, s32[8]{0:T(128)} %counts.1, s32[16,16]{1,0:T(8,128)} %send_list.1, bf16[1,8,128,512]{3,2,1,0:T(8,128)(2,1)} %bitcast.6, bf16[1,8,128,512]{3,2,1,0:T(8,128)(2,1)} %bitcast.7, bf16[3,8,128,512]{3,2,1,0:T(8,128)(2,1)} %bitcast.5, ...), custom_call_target="tpu_custom_call" | custom-call | tf_op jit(solution)/shard_map/pallas_call | solution.py:402
  105.7 2.0 %copy.10 = bf16[1,4,1024,512]{3,2,1,0:T(8,128)(2,1)} copy(bf16[1,4,1024,512]{3,2,1,0:T(8,128)(2,1)S(1)} %bitcast.4) | data formatting | bytes 8388608

commit v5 on v4

--- a/solution.py
+++ b/solution.py
@@ -33,11 +33,85 @@
     return math.log(1.0 + STRENGTH / (layer + 1))
 
 
-def kernel(n_section, n_x, n_z, col, counts, send_list, carry_h, carry_h0, new_h0, weights, adj, out, *scratch):
+def beta_of(section, n_section):
+    value = jnp.float32(beta_at(n_section - 1))
+    for s in range(n_section - 1):
+        value = jnp.where(section == s, jnp.float32(beta_at(s)), value)
+    return value
+
+
+def mixture_of(col, table, adjacency, anchor, r):
+    def entry(n):
+        return jnp.concatenate([table[c, n] for c in range(PER)], axis=1)
+
+    total = None
+    for k in range(adjacency.shape[1]):
+        picked = jnp.concatenate([entry(col[r, 2 * k]), entry(col[r, 2 * k + 1])], axis=0)
+        term = jnp.dot(adjacency[r, k], picked, preferred_element_type=jnp.float32)
+        total = term if total is None else total + term
+    return ((1.0 - TELEPORT) * total + TELEPORT * anchor.astype(jnp.float32)).astype(jnp.bfloat16)
+
+
+def layer_of(partial, right, weight, beta):
+    half = right.shape[1]
+    layer = partial + beta * jnp.dot(right, weight, preferred_element_type=jnp.float32)
+    layer = jnp.concatenate([layer[:, :half], layer[:, half:] + (1.0 - beta) * right.astype(jnp.float32)], axis=1)
+    return jnp.maximum(layer, 0.0).astype(jnp.bfloat16)
+
+
+def by_pairs(pairs, lines, mix, use, after):
+    def gather(g):
+        lines[g] = jnp.concatenate([mix(2 * g), mix(2 * g + 1)], axis=0)
+
+    def rows(g, carry):
+        use(g - 1, lines[g - 1])
+        gather(g)
+        after(g - 1)
+        return carry
+
+    gather(0)
+    lax.fori_loop(1, pairs, rows, 0)
+    use(pairs - 1, lines[pairs - 1])
+    after(pairs - 1)
+
+
+def last_kernel(n_section, col, done, table, held, partial, adjacency, weight, out, lines, result, done_sem, out_sem):
+    section = lax.axis_index("section")
+    last, blocks = STEPS - 1, result.shape[0]
+    half = lines.shape[2]
+    beta = beta_of(section, n_section)
+
+    def put(t):
+        return pltpu.make_async_copy(done.at[t], out.at[t], done_sem.at[t])
+
+    def leave(g):
+        rows = pl.ds(2 * g, 2)
+        return pltpu.make_async_copy(result.at[rows], out.at[last, rows], out_sem.at[g])
+
+    for t in range(last):
+        put(t).start()
+
+    def mix(r):
+        return mixture_of(col, table, adjacency, held[last, r, :, half:], r)
+
+    def use(g, right):
+        layer = layer_of(partial[g], right, weight[half:], beta)
+        for i in range(2):
+            result[2 * g + i] = layer[i * BLOCK : (i + 1) * BLOCK]
+
+    by_pairs(blocks // 2, lines, mix, use, lambda g: leave(g).start())
+    for t in range(last):
+        put(t).wait()
+    for g in range(blocks // 2):
+        leave(g).wait()
+
+
+def kernel(n_section, n_x, n_z, col, counts, send_list, carry_h, carry_h0, new_h0, weights, adj, out, last_table, held, partial, adjacency, weight, *scratch):
     owns, scratch = [scratch[t * CHUNKS : (t + 1) * CHUNKS] for t in range(STEPS)], scratch[STEPS * CHUNKS :]
-    tables, scratch = [scratch[t * HALVES : (t + 1) * HALVES] for t in range(STEPS)], scratch[STEPS * HALVES :]
+    tables, scratch = [*scratch[: STEPS * HALVES - 1], last_table], scratch[STEPS * HALVES - 1 :]
+    tables = [tables[t * HALVES : (t + 1) * HALVES] for t in range(STEPS)]
     (
-        outgoing, held, partial, lines, result, adjacency, weight,
+        outgoing, lines, result,
         token, load_sem, feed_sem, adj_sem, own_sem, send_sem, recv_sem, ship_send, ship_recv, held_send, held_recv,
     ) = scratch
     section = lax.axis_index("section")
@@ -200,43 +274,14 @@
         own_done(t, h).wait()
         arrived(t, h).wait()
 
-    def beta_of():
-        value = jnp.float32(beta_at(n_section - 1))
-        for s in range(n_section - 1):
-            value = jnp.where(section == s, jnp.float32(beta_at(s)), value)
-        return value
-
     def mix(t, h, r):
-        table = tables[t][h]
-
-        def entry(n):
-            return jnp.concatenate([table[c, n] for c in range(PER)], axis=1)
-
-        total = None
-        for k in range(slots // 2):
-            picked = jnp.concatenate([entry(col[r, 2 * k]), entry(col[r, 2 * k + 1])], axis=0)
-            term = jnp.dot(adjacency[r, k], picked, preferred_element_type=jnp.float32)
-            total = term if total is None else total + term
-        anchor = held[t, r, :, h * half : (h + 1) * half].astype(jnp.float32)
-        return ((1.0 - TELEPORT) * total + TELEPORT * anchor).astype(jnp.bfloat16)
+        return mixture_of(col, tables[t][h], adjacency, held[t, r, :, h * half : (h + 1) * half], r)
 
     def pipelined(t, h, use, after=lambda g: None):
-        def gather(g):
-            lines[g] = jnp.concatenate([mix(t, h, 2 * g), mix(t, h, 2 * g + 1)], axis=0)
-
-        def rows(g, carry):
-            use(g - 1, lines[g - 1])
-            gather(g)
-            after(g - 1)
-            return carry
-
-        gather(0)
-        lax.fori_loop(1, blocks // 2, rows, 0)
-        use(blocks // 2 - 1, lines[blocks // 2 - 1])
-        after(blocks // 2 - 1)
+        by_pairs(blocks // 2, lines, lambda r: mix(t, h, r), use, after)
 
     def begin(t):
-        beta = beta_of()
+        beta = beta_of(section, n_section)
 
         def use(g, left):
             product = beta * jnp.dot(left, weight[:half], preferred_element_type=jnp.float32)
@@ -246,20 +291,15 @@
         pipelined(t, 0, use)
 
     def finish(t):
-        beta = beta_of()
+        beta = beta_of(section, n_section)
 
         def use(g, right):
-            layer = partial[g] + beta * jnp.dot(right, weight[half:], preferred_element_type=jnp.float32)
-            layer = jnp.concatenate(
-                [layer[:, :half], layer[:, half:] + (1.0 - beta) * right.astype(jnp.float32)], axis=1
-            )
-            layer = jnp.maximum(layer, 0.0).astype(jnp.bfloat16)
+            layer = layer_of(partial[g], right, weight[half:], beta)
             for i in range(2):
                 rows_of = layer[i * BLOCK : (i + 1) * BLOCK]
                 out[t, 2 * g + i] = rows_of
-                if t < STEPS - 1:
-                    for c in range(CHUNKS):
-                        result[t, c, 2 * g + i] = rows_of[:, c * wide : (c + 1) * wide]
+                for c in range(CHUNKS):
+                    result[t, c, 2 * g + i] = rows_of[:, c * wide : (c + 1) * wide]
 
         def after(g):
             if t < STEPS - 1:
@@ -293,7 +333,8 @@
         wait_table(t, 1)
         if t == 2:
             let_in(2)
-        finish(t)
+        if t < STEPS - 1:
+            finish(t)
 
     def on(which, *work):
         @pl.when(core == which)
@@ -399,21 +440,28 @@
         scalars = pl.BlockSpec(memory_space=pltpu.SMEM)
         vmem = lambda *shape: pltpu.VMEM(shape, jnp.bfloat16)
         dma = lambda *shape: pltpu.SemaphoreType.DMA(shape)
-        out = pl.pallas_call(
+        inside = pl.BlockSpec(memory_space=pltpu.VMEM)
+        pair_sums = pltpu.VMEM((blocks // 2, 2 * BLOCK, width), jnp.float32)
+        kept = [
+            vmem(STEPS - 1, *tiles),
+            vmem(PER, blocks + n_dom, BLOCK, wide),
+            vmem(STEPS, *tiles),
+            pair_sums,
+            vmem(blocks, slots // 2, BLOCK, 2 * BLOCK),
+            vmem(width, width),
+        ]
+        lines = vmem(blocks // 2, 2 * BLOCK, width // HALVES)
+        kept = pl.pallas_call(
             functools.partial(kernel, n_section, n_x, n_z),
-            out_shape=vmem(STEPS, *tiles),
+            out_shape=kept,
             in_specs=[scalars] * 3 + [anywhere] * 5,
-            out_specs=pl.BlockSpec(memory_space=pltpu.VMEM),
+            out_specs=[inside] * len(kept),
             scratch_shapes=[vmem(blocks, BLOCK, wide)] * (STEPS * CHUNKS)
-            + [vmem(PER, blocks + n_dom, BLOCK, wide)] * (STEPS * HALVES)
+            + [vmem(PER, blocks + n_dom, BLOCK, wide)] * (STEPS * HALVES - 1)
             + [
                 vmem(STEPS, CHUNKS, PEERS, BLOCK, wide),
-                vmem(STEPS, *tiles),
-                pltpu.VMEM((blocks // 2, 2 * BLOCK, width), jnp.float32),
-                vmem(blocks // 2, 2 * BLOCK, width // HALVES),
+                lines,
                 vmem(STEPS - 1, CHUNKS, blocks, BLOCK, wide),
-                vmem(blocks, slots // 2, BLOCK, 2 * BLOCK),
-                vmem(width, width),
                 pltpu.SemaphoreType.REGULAR((3,)),
                 dma(3),
                 dma(2, STEPS - 1),
@@ -427,12 +475,20 @@
                 dma(STEPS),
             ],
             compiler_params=pltpu.CompilerParams(
-                collective_id=0, has_side_effects=True, vmem_limit_bytes=67_043_328 - (4 << 20) - (64 << 10)
+                collective_id=0, has_side_effects=True, vmem_limit_bytes=67_043_328 - (17 << 20) - (64 << 10)
             ),
         )(
             col_index, counts, send_list,
             carry_h.reshape(1, *tiles), carry_h0.reshape(1, *tiles), new_h0.reshape(-1, *tiles), weights, adj_blocks,
         )
+        out = pl.pallas_call(
+            functools.partial(last_kernel, n_section),
+            out_shape=jax.ShapeDtypeStruct((STEPS, *tiles), jnp.bfloat16),
+            in_specs=[scalars] + [inside] * len(kept),
+            out_specs=anywhere,
+            scratch_shapes=[lines, vmem(*tiles), dma(STEPS - 1), dma(blocks // 2)],
+            compiler_params=pltpu.CompilerParams(vmem_limit_bytes=8 << 20),
+        )(col_index, *kept)
         return out.reshape(1, STEPS, rows, width)
 
     in_specs = (

time: 108 us -> 108 us (level)
  local copies, waits for them, and re-layouts: 2.02 us -> 0.01 us
    pallas_call x0 -> x1, Pallas kernels: none -> 4.16 us  [body(): pl.pallas_call(functools.partial(last_kernel, n_section), out_shape=jax.S...]
    pallas_call x1, Pallas kernels: 106 us -> 103 us  [body(): pl.pallas_call(functools.partial(kernel, n_section, n_x, n_z), out_shape=...]
    unnamed x1 -> x2, local copies, waits for them, and re-layouts: 2.02 us -> 0.01 us
where the time goes in v5:
time: 108 us; the launch traced here: 107 us
  Pallas kernels  107 us (99%)
    pallas_call x1, Pallas kernels, body(): pl.pallas_call(functools.partial(kernel, n_section, n_x, n_z), out_shape=...  103 us
    pallas_call x1, Pallas kernels, body(): pl.pallas_call(functools.partial(last_kernel, n_section), out_shape=jax.S...  4.16 us

profile of v5, /device:TPU:16, one launch (start us, length us, event | category | flops | bytes accessed | tf_op | source)
XLA Modules:
  0.0 107.1 jit_solution(9434434518046871126)
XLA Ops:
  0.0 0.0 copy-start
  0.0 102.8 %shard_map.82 = (bf16[3,8,128,512]{3,2,1,0:T(8,128)(2,1)S(1)}, bf16[2,24,128,128]{3,2,1,0:T(8,128)(2,1)S(1)}, bf16[4,8,128,512]{3,2,1,0:T(8,128)(2,1)S(1)}, f32[...) custom-call(s32[8,24]{1,0:T(8,128)} %col.3, s32[8]{0:T(128)} %counts.1, ...), custom_call_target="tpu_custom_call" | custom-call | tf_op jit(solution)/shard_map/pallas_call | solution.py:454
  102.8 0.0 copy-done
  102.8 4.2 %shard_map.83 = bf16[4,8,128,512]{3,2,1,0:T(8,128)(2,1)} custom-call(s32[8,24]{1,0:T(8,128)S(1)} %copy-done, bf16[3,8,128,512]{3,2,1,0:T(8,128)(2,1)S(1)} %get-tuple-element.11.done, bf16[2,24,128,128]{3,2,1,0:T(8,128)(2,1)S(1)} %get-tuple-element.12.table, bf16[4,8,128,512]{3,2,1,0:T(8,128)(2,1)S(1)} %get-tuple-element.13.held, ...), custom_call_target="tpu_custom_call" | custom-call | tf_op jit(solution)/shard_map/pallas_call | solution.py:484
Async XLA Ops:
  0.0 102.8 %copy-start = (s32[8,24]{1,0:T(8,128)S(1)}, s32[8,24]{1,0:T(8,128)}, u32[]{:S(2)}) copy-start(s32[8,24]{1,0:T(8,128)} %col.3) | copy-start | bytes 2308
